TPU v7x, 32 devices: a whole 2x2x4 slice. The times are simulated.
32 devices in a mesh: nest: 4 (over x, core), py: 2 (over y), px: 4 (over z).
Axes of the slice: x: 2, y: 2, z: 4, core: 2. Of those that a mesh axis runs over, the one named last changes fastest.
Arguments:
- initial_state: float32 [4, 4, 256, 256], P('nest', None, 'px', 'py'), may hold values from -6 to 6
- drive_modes: float32 [3, 4, 64, 64], replicated, may hold values from -6 to 6
- relax_rates: float32 [4, 4], P('nest'), may hold values from 0.2 to 0.9
- nest_offsets: int32 [4, 2], replicated, may hold values from 0 to 170
Outputs:
- final_state: float32 [4, 4, 256, 256], P('nest', None, 'px', 'py')
- final_modes: float32 [4, 4, 64, 64], P('nest')
Inputs may be any that keep to these rules, and one draw needn't show every extreme that they name: `nest_offsets`: row 0 is not read.
All inputs are finite; a program needn't handle non-finite values.
Results may differ from a plain program's by a relative error of at most 0.0001.
Values sent between devices are 32-bit elements; how exact they have to be, the bound alone decides.
A program may use at most 64 MiB of HBM per device.

v0:
```python
import math
import jax
import jax.numpy as jnp
import numpy as np
from jax import lax
from jax.sharding import PartitionSpec as P

RATIO = 3
RATE = 0.2
HI = lax.Precision.HIGHEST


def basis(cells, modes, refine, fn=np.cos):
    j = np.arange(modes, dtype=np.int64)
    q = 2 * np.arange(cells, dtype=np.int64) + 1
    product = j[None, :] * q[:, None] % (4 * refine * cells)
    weight = np.where(j == 0, 1.0, 2.0) / cells
    return np.sqrt(weight)[None, :] * fn(np.pi * product / (2.0 * refine * cells))


def half_step(table):
    pad = np.pad(table, ((1, 1), (0, 0)))
    return (0.5 - 2 * RATE) * table + RATE * (pad[2:] + pad[:-2])


def powers(table, count):
    out = [table]
    for _ in range(count):
        out.append(half_step(out[-1]))
    return out


def offset_map(cells, modes, offset):
    base = basis(cells, modes, 1)
    even = jnp.asarray(base.T @ basis(cells, modes, RATIO), jnp.float32)
    odd = jnp.asarray(base.T @ basis(cells, modes, RATIO, np.sin), jnp.float32)
    j = jnp.arange(modes, dtype=jnp.int32)
    product = j * (2 * RATIO * offset) % (4 * RATIO * cells)
    angle = jnp.pi * product.astype(jnp.float32) / (2.0 * RATIO * cells)
    return even * jnp.cos(angle)[None, :] - odd * jnp.sin(angle)[None, :]


def exchange(value, axis, dim, width):
    n, length = (lax.axis_size(axis), value.shape[dim])
    up = [(i, i + 1) for i in range(n - 1)]
    down = [(i + 1, i) for i in range(n - 1)]
    before = lax.ppermute(lax.slice_in_dim(value, length - width, length, axis=dim), axis, up)
    after = lax.ppermute(lax.slice_in_dim(value, 0, width, axis=dim), axis, down)
    return jnp.concatenate([before, value, after], axis=dim)


def free_steps(field, total_x, total_y, steps):
    levels, cx, cy = field.shape
    pad = exchange(exchange(field, "py", 2, steps), "px", 1, steps)
    gx = lax.axis_index("px") * cx - steps + jnp.arange(cx + 2 * steps)
    gy = lax.axis_index("py") * cy - steps + jnp.arange(cy + 2 * steps)
    inside = ((gx >= 0) & (gx < total_x))[:, None] & ((gy >= 0) & (gy < total_y))[None, :]
    for s in range(steps):
        mid = pad[:, 1:-1, 1:-1]
        near = pad[:, 2:, 1:-1] + pad[:, :-2, 1:-1] + pad[:, 1:-1, 2:] + pad[:, 1:-1, :-2]
        pad = mid + RATE * (near - 4.0 * mid)
        cut = s + 1
        pad = jnp.where(inside[cut:-cut, cut:-cut][None], pad, 0.0)
    return pad


def body(initial_state, drive_modes, relax_rates, nest_offsets):
    k = lax.axis_index("nest")
    nests = lax.axis_size("nest")
    field = initial_state[0]
    levels, cx, cy = field.shape
    windows, _, m, _ = drive_modes.shape
    nx, ny = (cx * lax.axis_size("px"), cy * lax.axis_size("py"))
    rp, cp = (powers(basis(nx, m, 1), windows), powers(basis(ny, m, 1), windows))
    a = [jnp.asarray(rp[0].T @ t, jnp.float32) for t in rp]
    b = [jnp.asarray(cp[0].T @ t, jnp.float32) for t in cp]
    u_all = jnp.asarray(np.concatenate(rp, 1), jnp.float32)
    v_all = jnp.asarray(np.concatenate(cp, 1), jnp.float32)
    u = lax.dynamic_slice_in_dim(u_all, lax.axis_index("px") * cx, cx, 0)
    v = lax.dynamic_slice_in_dim(v_all, lax.axis_index("py") * cy, cy, 0)
    half = jnp.einsum("lxy,yq->lxq", field, v, precision=HI)
    rows = []
    for w in range(1, windows + 1):
        terms = [math.comb(w, i) * half[:, :, (w - i) * m : (w - i + 1) * m] for i in range(w + 1)]
        rows.append(
            jnp.einsum(
                "xj,lxm->ljm",
                jnp.concatenate([u[:, i * m : (i + 1) * m] for i in range(w + 1)], 0),
                jnp.concatenate(terms, 1),
                precision=HI,
            )
        )
    shares = lax.psum(jnp.stack(rows), ("py", "px"))
    gain = relax_rates[0][:, None, None]
    row_map = offset_map(nx, m, nest_offsets[k, 0])
    col_map = offset_map(ny, m, nest_offsets[k, 1])

    def left(t, x):
        return jnp.einsum("jp,lpq->ljq", t, x, precision=HI)

    def right(x, t):
        return jnp.einsum("ljq,mq->ljm", x, t, precision=HI)

    def spread(d, x):
        out = left(a[d], x) + right(x, b[d])
        for i in range(1, d):
            out = out + math.comb(d, i) * right(left(a[i], x), b[d - i])
        return out

    parent = jnp.zeros_like(drive_modes)
    for stage in range(nests):
        if stage:
            parent = lax.ppermute(coeffs, "nest", [(i, i + 1) for i in range(nests - 1)])
            interp = jnp.einsum("jp,wlpq->wljq", row_map, parent, precision=HI)
            interp = jnp.einsum("wljq,mq->wljm", interp, col_map, precision=HI)
            target = jnp.where(k == 0, drive_modes, interp)
        else:
            target = drive_modes
        changes, kept = ([], [])
        for w in range(windows):
            own = shares[w]
            for e in range(w):
                own = own + spread(w - e, changes[e])
            changes.append(gain * (target[w] - own))
            kept.append(own + changes[-1])
        coeffs = jnp.stack(kept)
    free = free_steps(field, nx, ny, windows)
    zero = jnp.zeros_like(changes[0])
    blocks = [
        jnp.concatenate(
            [
                math.comb(i + j, i) * changes[windows - 1 - i - j] if i + j < windows else zero
                for j in range(windows)
            ],
            2,
        )
        for i in range(windows)
    ]
    mixed = jnp.concatenate(blocks, 1)
    wide = windows * m
    back = jnp.einsum("lpq,yq->lpy", mixed, v[:, :wide], precision=HI)
    final = free + jnp.einsum("xp,lpy->lxy", u[:, :wide], back, precision=HI)
    return (final[None], coeffs[windows - 1][None])


def solution(mesh):
    spec = P("nest", None, "px", "py")
    return jax.shard_map(
        body,
        mesh=mesh,
        in_specs=(spec, P(), P("nest", None), P()),
        out_specs=(spec, P("nest", None, None, None)),
        check_vma=False,
    )
```

profile of v0, /device:TPU:1, one launch (start us, length us, event | category | flops | bytes accessed | tf_op | source)
XLA Modules:
  0.0 136.2 jit_solution(14306321260385565725)
XLA Ops:
  7.2 1.3 convolution_bitcast_fusion.3
  8.7 0.8 copy-done.7
  9.6 0.3 convolution_bitcast_fusion.19
  9.9 0.4 convolution_bitcast_fusion.6
  10.4 0.5 convolution_bitcast_fusion.5
  10.8 0.8 pad_maximum_fusion
  11.7 0.9 copy-done.3
  12.6 4.1 %collective-permute-start = (f32[4,64,3]{2,1,0:T(8,128)S(1)}, f32[4,64,3]{2,1,0:T(8,128)S(1)}, u32[]{:S(2)}, u32[]{:S(2)}) collective-permute-start(f32[4,64,3]{2,1,0:T(8,128)S(1)} %get-tuple-element.23), channel_id=1, source_target_pairs={{0,4},{1,5},{2,6},{3,7},{8,12},{9,13},{10,14},{11,15},{16,20},{17,... | collective-permute-start | bytes 9224 | tf_op jit(solution)/shard_map/ppermute | solution.py:47
  16.7 1.3 collective-permute-start.1
  18.1 0.7 copy-done.9
  18.8 0.6 constant_dynamic-slice_fusion.2
  20.8 4.1 %collective-permute-done.1 = f32[4,64,3]{2,1,0:T(8,128)S(1)} collective-permute-done((f32[4,64,3]{2,1,0:T(8,128)S(1)}, f32[4,64,3]{2,1,0:T(8,128)S(1)}, u32[]{:S(2)}, u32[]{:S(2)}) %collective-permute-start.1) | collective-permute-done | bytes 3104 | tf_op jit(solution)/shard_map/ppermute | solution.py:48
  25.0 3.2 %collective-permute-start.2 = (f32[4,3,134]{2,1,0:T(4,128)S(1)}, f32[4,3,134]{2,1,0:T(4,128)S(1)}, u32[]{:S(2)}, u32[]{:S(2)}) collective-permute-start(f32[4,3,134]{2,1,0:T(4,128)S(1)} %get-tuple-element.10), channel_id=1, source_target_pairs={{0,1},{1,2},{2,3},{4,5},{5,6},{6,7},{8,9},{9,10},{10,11},{12,13},{... | collective-permute-start | bytes 19304 | tf_op jit(solution)/shard_map/ppermute | solution.py:47
  28.3 1.3 collective-permute-start.3
  29.6 54.6 %all-reduce.3.cloned.1.call-done = f32[3,4,64,64]{3,2,1,0:T(8,128)} async-done(((f32[3,4,64,64]{3,2,1,0:T(8,128)}), f32[3,4,64,64]{3,2,1,0:T(8,128)}) %all-reduce.3.cloned.1.call-update) | async-done | bytes 196624 | tf_op jit(solution)/shard_map/psum | solution.py:93
  84.3 1.0 bitcast_multiply_fusion.2
  85.8 0.4 copy-done.2
  86.5 0.3 convolution_bitcast_fusion.16
  87.0 0.3 convolution_add_fusion.9
  87.3 0.4 copy-done.4
  88.4 5.6 %collective-permute-start.4 = (f32[3,4,64,64]{3,2,1,0:T(8,128)S(1)}, f32[3,4,64,64]{3,2,1,0:T(8,128)S(1)}, u32[]{:S(2)}, u32[]{:S(2)}) collective-permute-start(f32[3,4,64,64]{3,2,1,0:T(8,128)S(1)} %pad_maximum_fusion.1), channel_id=1, source_target_pairs={{0,8},{8,16},{16,24},{1,9},{9,17},{17,25},{2,10},{10,18},{18,26},{... | collective-permute-start | bytes 589832 | tf_op jit(solution)/shard_map/ppermute | solution.py:113
  94.7 4.1 %collective-permute-done.4 = f32[3,4,64,64]{3,2,1,0:T(8,128)S(1)} collective-permute-done((f32[3,4,64,64]{3,2,1,0:T(8,128)S(1)}, f32[3,4,64,64]{3,2,1,0:T(8,128)S(1)}, u32[]{:S(2)}, u32[]{:S(2)}) %collective-permute-start.4) | collective-permute-done | bytes 196640 | tf_op jit(solution)/shard_map/ppermute | solution.py:113
  98.8 0.5 convolution_bitcast_fusion.2
  99.3 0.5 convolution_select_fusion.2
  99.8 0.3 convolution_bitcast_fusion.15
  100.2 0.3 fusion.6
  100.6 0.3 convolution_bitcast_fusion.13
  101.2 0.3 convolution_bitcast_fusion.14
  101.8 0.3 fusion.71
  102.2 4.4 %collective-permute-start.5 = (f32[3,4,64,64]{3,2,1,0:T(8,128)S(1)}, f32[3,4,64,64]{3,2,1,0:T(8,128)S(1)}, u32[]{:S(2)}, u32[]{:S(2)}) collective-permute-start(f32[3,4,64,64]{3,2,1,0:T(8,128)S(1)} %pad_maximum_fusion.2), channel_id=1, source_target_pairs={{0,8},{8,16},{16,24},{1,9},{9,17},{17,25},{2,10},{10,18},{18,26},{... | collective-permute-start | bytes 589832 | tf_op jit(solution)/shard_map/ppermute | solution.py:113
  106.6 0.4 fusion.54
  107.0 4.3 %collective-permute-done.5 = f32[3,4,64,64]{3,2,1,0:T(8,128)S(1)} collective-permute-done((f32[3,4,64,64]{3,2,1,0:T(8,128)S(1)}, f32[3,4,64,64]{3,2,1,0:T(8,128)S(1)}, u32[]{:S(2)}, u32[]{:S(2)}) %collective-permute-start.5) | collective-permute-done | bytes 196640 | tf_op jit(solution)/shard_map/ppermute | solution.py:113
  111.3 0.5 convolution_bitcast_fusion.1
  111.8 0.5 convolution_select_fusion.1
  112.4 0.3 convolution_bitcast_fusion.12
  112.7 0.3 fusion.10
  113.1 0.3 convolution_bitcast_fusion.10
  113.8 0.3 convolution_bitcast_fusion.11
  114.1 0.3 convolution_add_fusion.3
  114.4 0.3 fusion.65
  114.8 4.6 %collective-permute-start.6 = (f32[3,4,64,64]{3,2,1,0:T(8,128)S(1)}, f32[3,4,64,64]{3,2,1,0:T(8,128)S(1)}, u32[]{:S(2)}, u32[]{:S(2)}) collective-permute-start(f32[3,4,64,64]{3,2,1,0:T(8,128)S(1)} %pad_maximum_fusion.3), channel_id=1, source_target_pairs={{0,8},{8,16},{16,24},{1,9},{9,17},{17,25},{2,10},{10,18},{18,26},{... | collective-permute-start | bytes 589832 | tf_op jit(solution)/shard_map/ppermute | solution.py:113
  119.4 0.4 fusion.50
  119.8 4.1 %collective-permute-done.6 = f32[3,4,64,64]{3,2,1,0:T(8,128)S(1)} collective-permute-done((f32[3,4,64,64]{3,2,1,0:T(8,128)S(1)}, f32[3,4,64,64]{3,2,1,0:T(8,128)S(1)}, u32[]{:S(2)}, u32[]{:S(2)}) %collective-permute-start.6) | collective-permute-done | bytes 196640 | tf_op jit(solution)/shard_map/ppermute | solution.py:113
  123.9 0.5 convolution_bitcast_fusion
  124.4 0.5 convolution_select_fusion
  126.6 0.9 add_bitcast_fusion
  127.5 0.8 fusion.20
  128.4 1.0 fusion.1
  (59 shorter events, 5.6 us)
Async XLA Ops:
  7.2 77.1 %all-reduce.3.cloned.1.call-start = ((), (), s32[]{:S(2)}) async-start(), calls=%async_computation | async-start | bytes 786432 | tf_op jit(solution)/shard_map/psum | solution.py:93
  8.6 1.0 copy-start.7
  11.6 0.9 copy-start.3
  12.5 71.7 %copy-start.1 = (f32[3,4,64,64]{3,2,1,0:T(8,128)S(1)}, f32[3,4,64,64]{3,2,1,0:T(8,128)}, u32[]{:S(2)}) copy-start(f32[3,4,64,64]{3,2,1,0:T(8,128)} %param.15) | copy-start | bytes 589828
  12.6 8.2 %collective-permute-start = (f32[4,64,3]{2,1,0:T(8,128)S(1)}, f32[4,64,3]{2,1,0:T(8,128)S(1)}, u32[]{:S(2)}, u32[]{:S(2)}) collective-permute-start(f32[4,64,3]{2,1,0:T(8,128)S(1)} %get-tuple-element.23), channel_id=1, source_target_pairs={{0,4},{1,5},{2,6},{3,7},{8,12},{9,13},{10,14},{11,15},{16,20},{17,... | collective-permute-start | bytes 9224 | tf_op jit(solution)/shard_map/ppermute | solution.py:47
  16.7 8.2 %collective-permute-start.1 = (f32[4,64,3]{2,1,0:T(8,128)S(1)}, f32[4,64,3]{2,1,0:T(8,128)S(1)}, u32[]{:S(2)}, u32[]{:S(2)}) collective-permute-start(f32[4,64,3]{2,1,0:T(8,128)S(1)} %get-tuple-element.24), channel_id=1, source_target_pairs={{4,0},{5,1},{6,2},{7,3},{12,8},{13,9},{14,10},{15,11},{20,16},{21,... | collective-permute-start | bytes 9224 | tf_op jit(solution)/shard_map/ppermute | solution.py:48
  18.1 0.7 copy-start.9
  25.0 69.4 %collective-permute-start.2 = (f32[4,3,134]{2,1,0:T(4,128)S(1)}, f32[4,3,134]{2,1,0:T(4,128)S(1)}, u32[]{:S(2)}, u32[]{:S(2)}) collective-permute-start(f32[4,3,134]{2,1,0:T(4,128)S(1)} %get-tuple-element.10), channel_id=1, source_target_pairs={{0,1},{1,2},{2,3},{4,5},{5,6},{6,7},{8,9},{9,10},{10,11},{12,13},{... | collective-permute-start | bytes 19304 | tf_op jit(solution)/shard_map/ppermute | solution.py:47
  28.3 56.0 %copy-start.8 = (f32[1,4]{1,0:T(1,128)S(1)}, f32[1,4]{1,0:T(1,128)}, u32[]{:S(2)}) copy-start(f32[1,4]{1,0:T(1,128)} %param.16) | copy-start | bytes 52
  28.3 66.2 %collective-permute-start.3 = (f32[4,3,134]{2,1,0:T(4,128)S(1)}, f32[4,3,134]{2,1,0:T(4,128)S(1)}, u32[]{:S(2)}, u32[]{:S(2)}) collective-permute-start(f32[4,3,134]{2,1,0:T(4,128)S(1)} %get-tuple-element.11), channel_id=1, source_target_pairs={{1,0},{2,1},{3,2},{5,4},{6,5},{7,6},{9,8},{10,9},{11,10},{13,12},{... | collective-permute-start | bytes 19304 | tf_op jit(solution)/shard_map/ppermute | solution.py:48
  84.3 1.0 copy-start
  85.3 1.0 copy-start.2
  87.0 0.8 copy-start.4
  88.4 10.3 %collective-permute-start.4 = (f32[3,4,64,64]{3,2,1,0:T(8,128)S(1)}, f32[3,4,64,64]{3,2,1,0:T(8,128)S(1)}, u32[]{:S(2)}, u32[]{:S(2)}) collective-permute-start(f32[3,4,64,64]{3,2,1,0:T(8,128)S(1)} %pad_maximum_fusion.1), channel_id=1, source_target_pairs={{0,8},{8,16},{16,24},{1,9},{9,17},{17,25},{2,10},{10,18},{18,26},{... | collective-permute-start | bytes 589832 | tf_op jit(solution)/shard_map/ppermute | solution.py:113
  94.4 4.3 %copy-start.5 = (f32[64,64]{1,0:T(8,128)S(1)}, f32[64,64]{1,0:T(8,128)}, u32[]{:S(2)}) copy-start(f32[64,64]{1,0:T(8,128)} %constant.86.clone) | copy-start | bytes 49156
  94.5 4.3 %copy-start.6 = (f32[64,64]{1,0:T(8,128)S(1)}, f32[64,64]{1,0:T(8,128)}, u32[]{:S(2)}) copy-start(f32[64,64]{1,0:T(8,128)} %constant.87.clone) | copy-start | bytes 49156
  102.2 9.1 %collective-permute-start.5 = (f32[3,4,64,64]{3,2,1,0:T(8,128)S(1)}, f32[3,4,64,64]{3,2,1,0:T(8,128)S(1)}, u32[]{:S(2)}, u32[]{:S(2)}) collective-permute-start(f32[3,4,64,64]{3,2,1,0:T(8,128)S(1)} %pad_maximum_fusion.2), channel_id=1, source_target_pairs={{0,8},{8,16},{16,24},{1,9},{9,17},{17,25},{2,10},{10,18},{18,26},{... | collective-permute-start | bytes 589832 | tf_op jit(solution)/shard_map/ppermute | solution.py:113
  114.8 9.1 %collective-permute-start.6 = (f32[3,4,64,64]{3,2,1,0:T(8,128)S(1)}, f32[3,4,64,64]{3,2,1,0:T(8,128)S(1)}, u32[]{:S(2)}, u32[]{:S(2)}) collective-permute-start(f32[3,4,64,64]{3,2,1,0:T(8,128)S(1)} %pad_maximum_fusion.3), channel_id=1, source_target_pairs={{0,8},{8,16},{16,24},{1,9},{9,17},{17,25},{2,10},{10,18},{18,26},{... | collective-permute-start | bytes 589832 | tf_op jit(solution)/shard_map/ppermute | solution.py:113
Sparse Core Ops, SparseCore 0:
  11.8 72.4 all-reduce.2
where the time goes:
time: 137 us; the launch traced here: 136 us
  waiting for transfers between devices  71.3 us (52%)
  starting transfers between devices  24.6 us (18%)
  matrix products  16.2 us (12%)
  between operations  16 us (12%)
  local copies, waits for them, and re-layouts  4.31 us (3%)
  other arithmetic  3.84 us (3%)
    psum x1, waiting for transfers between devices, body(): shares = lax.psum(jnp.stack(rows), ('py', 'px'))  54.6 us
    ppermute x3, starting transfers between devices, body(): lax.ppermute(coeffs, 'nest', [(i, i + 1) for i in range(nests - 1)])  14.6 us
    ppermute x3, waiting for transfers between devices, body(): lax.ppermute(coeffs, 'nest', [(i, i + 1) for i in range(nests - 1)])  12.5 us
    ppermute x2, starting transfers between devices, exchange(): lax.ppermute(lax.slice_in_dim(value, length - width, length, axis=dim), a...  7.35 us
    dot_general x16, matrix products, right(): return jnp.einsum('ljq,mq->ljm', x, t, precision=HI)  5.31 us
    ppermute x2, waiting for transfers between devices, exchange(): lax.ppermute(lax.slice_in_dim(value, 0, width, axis=dim), axis, down)  4.13 us
    dot_general x12, matrix products, left(): return jnp.einsum('jp,lpq->ljq', t, x, precision=HI)  3.66 us
    unnamed x20, local copies, waits for them, and re-layouts  3.27 us
  transfers between devices with their start and end apart: 8, of which 5 were waited for; matrix products, arithmetic and copies ran while one was open for 4% of the time, Pallas kernels for 0%

commit v1 on v0

--- a/solution.py
+++ b/solution.py
@@ -4,10 +4,12 @@
 import numpy as np
 from jax import lax
 from jax.sharding import PartitionSpec as P
+from jax.lax import all_gather
 
 RATIO = 3
 RATE = 0.2
 HI = lax.Precision.HIGHEST
+_tell_targets = lambda local_values: jnp.sum(all_gather(local_values, ("py", "px")), 0)
 
 
 def basis(cells, modes, refine, fn=np.cos):
@@ -90,7 +92,7 @@
                 precision=HI,
             )
         )
-    shares = lax.psum(jnp.stack(rows), ("py", "px"))
+    shares = _tell_targets(jnp.stack(rows))
     gain = relax_rates[0][:, None, None]
     row_map = offset_map(nx, m, nest_offsets[k, 0])
     col_map = offset_map(ny, m, nest_offsets[k, 1])

time: 137 us -> 127 us (0.927)
  waiting for transfers between devices: 71.3 us -> 61.6 us
  local copies, waits for them, and re-layouts: 4.31 us -> 2.88 us
    psum x1 -> x0, waiting for transfers between devices: 54.6 us -> none  [body(): shares = lax.psum(jnp.stack(rows), ('py', 'px'))]
    all_gather x0 -> x1, waiting for transfers between devices: none -> 46.7 us  [all_gather(local_values, ('py', 'px'))]
    unnamed x20 -> x18, local copies, waits for them, and re-layouts: 3.27 us -> 0.05 us
    reduce_sum x0 -> x1, other arithmetic: none -> 2.28 us  [jnp.sum(all_gather(local_values, ('py', 'px')), 0)]
    ppermute x2, waiting for transfers between devices: 4.13 us -> 2.31 us  [exchange(): lax.ppermute(lax.slice_in_dim(value, 0, width, axis=dim), axis, down)]
  transfers between devices with their start and end apart: 8 -> 8, of which waited for: 5 -> 5; matrix products, arithmetic and copies ran while one was open for 4% -> 5% of each run, Pallas kernels for 0% -> 0%
where the time goes in v1:
time: 127 us
  waiting for transfers between devices  61.6 us (49%)
  starting transfers between devices  24.2 us (19%)
  matrix products  17.5 us (14%)
  between operations  16 us (13%)
  other arithmetic  4.44 us (3%)
  local copies, waits for them, and re-layouts  2.88 us (2%)
    all_gather x1, waiting for transfers between devices, all_gather(local_values, ('py', 'px'))  46.7 us
    ppermute x3, starting transfers between devices, body(): lax.ppermute(coeffs, 'nest', [(i, i + 1) for i in range(nests - 1)])  14.4 us
    ppermute x3, waiting for transfers between devices, body(): lax.ppermute(coeffs, 'nest', [(i, i + 1) for i in range(nests - 1)])  12.6 us
    ppermute x2, starting transfers between devices, exchange(): lax.ppermute(lax.slice_in_dim(value, length - width, length, axis=dim), a...  7.15 us
    dot_general x16, matrix products, right(): return jnp.einsum('ljq,mq->ljm', x, t, precision=HI)  5.31 us
    dot_general x12, matrix products, left(): return jnp.einsum('jp,lpq->ljq', t, x, precision=HI)  3.68 us
    ppermute x2, starting transfers between devices, exchange(): lax.ppermute(lax.slice_in_dim(value, 0, width, axis=dim), axis, down)  2.58 us
  transfers between devices with their start and end apart: 8, of which 5 were waited for; matrix products, arithmetic and copies ran while one was open for 5% of the time, Pallas kernels for 0%

profile of v1, /device:TPU:1, one launch (start us, length us, event | category | flops | bytes accessed | tf_op | source)
XLA Modules:
  0.0 126.6 jit_solution(2207021630502635592)
XLA Ops:
  7.2 1.4 %convolution_bitcast_fusion.3 = f32[4,64,256]{2,1,0:T(8,128)S(1)} fusion(f32[256,256]{1,0:T(8,128)} %constant.85.clone, s32[]{:T(128)S(6)} %select_n.67, f32[1,4,64,128]{3,2,1,0:T(8,128)} %param.14), kind=kOutput, calls=%fused_computation.6 | convolution fusion | flops 100663296 | bytes 524292 | tf_op jit(solution)/shard_map/lxy,yq->lxq/dot_general | solution.py:83
  8.8 1.0 constant_dynamic-slice_fusion
  9.7 0.6 convolution_bitcast_fusion.19
  10.3 0.8 convolution_bitcast_fusion.6
  11.1 1.0 convolution_bitcast_fusion.5
  12.2 0.9 copy.46
  13.3 4.0 %collective-permute-start = (f32[4,64,3]{2,1,0:T(8,128)S(1)}, f32[4,64,3]{2,1,0:T(8,128)S(1)}, u32[]{:S(2)}, u32[]{:S(2)}) collective-permute-start(f32[4,64,3]{2,1,0:T(8,128)S(1)} %get-tuple-element.23), channel_id=1, source_target_pairs={{0,4},{1,5},{2,6},{3,7},{8,12},{9,13},{10,14},{11,15},{16,20},{17,... | collective-permute-start | bytes 9224 | tf_op jit(solution)/shard_map/ppermute | solution.py:49
  17.2 1.3 %collective-permute-start.1 = (f32[4,64,3]{2,1,0:T(8,128)S(1)}, f32[4,64,3]{2,1,0:T(8,128)S(1)}, u32[]{:S(2)}, u32[]{:S(2)}) collective-permute-start(f32[4,64,3]{2,1,0:T(8,128)S(1)} %get-tuple-element.24), channel_id=1, source_target_pairs={{4,0},{5,1},{6,2},{7,3},{12,8},{13,9},{14,10},{15,11},{20,16},{21,... | collective-permute-start | bytes 9224 | tf_op jit(solution)/shard_map/ppermute | solution.py:50
  18.5 0.6 constant_dynamic-slice_fusion.2
  20.6 2.3 %collective-permute-done.1 = f32[4,64,3]{2,1,0:T(8,128)S(1)} collective-permute-done((f32[4,64,3]{2,1,0:T(8,128)S(1)}, f32[4,64,3]{2,1,0:T(8,128)S(1)}, u32[]{:S(2)}, u32[]{:S(2)}) %collective-permute-start.1) | collective-permute-done | bytes 3104 | tf_op jit(solution)/shard_map/ppermute | solution.py:50
  23.0 3.2 %collective-permute-start.2 = (f32[4,3,134]{2,1,0:T(4,128)S(1)}, f32[4,3,134]{2,1,0:T(4,128)S(1)}, u32[]{:S(2)}, u32[]{:S(2)}) collective-permute-start(f32[4,3,134]{2,1,0:T(4,128)S(1)} %get-tuple-element.10), channel_id=1, source_target_pairs={{0,1},{1,2},{2,3},{4,5},{5,6},{6,7},{8,9},{9,10},{10,11},{12,13},{... | collective-permute-start | bytes 19304 | tf_op jit(solution)/shard_map/ppermute | solution.py:49
  26.2 1.3 %collective-permute-start.3 = (f32[4,3,134]{2,1,0:T(4,128)S(1)}, f32[4,3,134]{2,1,0:T(4,128)S(1)}, u32[]{:S(2)}, u32[]{:S(2)}) collective-permute-start(f32[4,3,134]{2,1,0:T(4,128)S(1)} %get-tuple-element.11), channel_id=1, source_target_pairs={{1,0},{2,1},{3,2},{5,4},{6,5},{7,6},{9,8},{10,9},{11,10},{13,12},{... | collective-permute-start | bytes 19304 | tf_op jit(solution)/shard_map/ppermute | solution.py:50
  27.5 46.7 %all-gather.3.cloned.1.call-done = f32[24,4,64,64]{3,2,1,0:T(8,128)} async-done(((f32[3,4,64,64]{3,2,1,0:T(8,128)}), f32[24,4,64,64]{3,2,1,0:T(8,128)}) %all-gather.3.cloned.1.call-update) | async-done | bytes 1572880 | tf_op jit(solution)/shard_map/all_gather | solution.py:12
  74.2 2.3 %reduce_sum.9 = f32[3,4,64,64]{3,2,1,0:T(8,128)S(1)} reduce(f32[8,3,4,64,64]{4,3,2,1,0:T(8,128)} %bitcast.271, f32[]{:T(128)} %constant.37.clone.1), dimensions={0}, to_apply=%region_0.0 | reduce | flops 344064 | bytes 1769476 | tf_op jit(solution)/shard_map/reduce_sum | solution.py:12
  76.9 0.3 fusion.2
  77.5 0.3 convolution_bitcast_fusion.16
  78.0 0.3 convolution_add_fusion.9
  78.6 0.3 fusion.86
  78.9 5.4 %collective-permute-start.4 = (f32[3,4,64,64]{3,2,1,0:T(8,128)S(1)}, f32[3,4,64,64]{3,2,1,0:T(8,128)S(1)}, u32[]{:S(2)}, u32[]{:S(2)}) collective-permute-start(f32[3,4,64,64]{3,2,1,0:T(8,128)S(1)} %pad_maximum_fusion.1), channel_id=1, source_target_pairs={{0,8},{8,16},{16,24},{1,9},{9,17},{17,25},{2,10},{10,18},{18,26},{... | collective-permute-start | bytes 589832 | tf_op jit(solution)/shard_map/ppermute | solution.py:115
  84.9 4.1 %collective-permute-done.4 = f32[3,4,64,64]{3,2,1,0:T(8,128)S(1)} collective-permute-done((f32[3,4,64,64]{3,2,1,0:T(8,128)S(1)}, f32[3,4,64,64]{3,2,1,0:T(8,128)S(1)}, u32[]{:S(2)}, u32[]{:S(2)}) %collective-permute-start.4) | collective-permute-done | bytes 196640 | tf_op jit(solution)/shard_map/ppermute | solution.py:115
  89.1 0.5 convolution_bitcast_fusion.2
  89.6 0.5 convolution_select_fusion.2
  90.1 0.3 convolution_bitcast_fusion.15
  90.5 0.3 fusion.6
  90.9 0.3 convolution_bitcast_fusion.13
  91.5 0.3 convolution_bitcast_fusion.14
  91.8 0.3 convolution_add_fusion.6
  92.2 0.3 fusion.71
  92.5 4.4 %collective-permute-start.5 = (f32[3,4,64,64]{3,2,1,0:T(8,128)S(1)}, f32[3,4,64,64]{3,2,1,0:T(8,128)S(1)}, u32[]{:S(2)}, u32[]{:S(2)}) collective-permute-start(f32[3,4,64,64]{3,2,1,0:T(8,128)S(1)} %pad_maximum_fusion.2), channel_id=1, source_target_pairs={{0,8},{8,16},{16,24},{1,9},{9,17},{17,25},{2,10},{10,18},{18,26},{... | collective-permute-start | bytes 589832 | tf_op jit(solution)/shard_map/ppermute | solution.py:115
  96.9 0.4 fusion.54
  97.3 4.3 %collective-permute-done.5 = f32[3,4,64,64]{3,2,1,0:T(8,128)S(1)} collective-permute-done((f32[3,4,64,64]{3,2,1,0:T(8,128)S(1)}, f32[3,4,64,64]{3,2,1,0:T(8,128)S(1)}, u32[]{:S(2)}, u32[]{:S(2)}) %collective-permute-start.5) | collective-permute-done | bytes 196640 | tf_op jit(solution)/shard_map/ppermute | solution.py:115
  101.6 0.5 convolution_bitcast_fusion.1
  102.1 0.5 convolution_select_fusion.1
  102.7 0.3 convolution_bitcast_fusion.12
  103.0 0.3 fusion.10
  103.4 0.3 convolution_bitcast_fusion.10
  104.1 0.3 convolution_bitcast_fusion.11
  104.4 0.3 convolution_add_fusion.3
  104.7 0.3 fusion.65
  105.1 4.6 %collective-permute-start.6 = (f32[3,4,64,64]{3,2,1,0:T(8,128)S(1)}, f32[3,4,64,64]{3,2,1,0:T(8,128)S(1)}, u32[]{:S(2)}, u32[]{:S(2)}) collective-permute-start(f32[3,4,64,64]{3,2,1,0:T(8,128)S(1)} %pad_maximum_fusion.3), channel_id=1, source_target_pairs={{0,8},{8,16},{16,24},{1,9},{9,17},{17,25},{2,10},{10,18},{18,26},{... | collective-permute-start | bytes 589832 | tf_op jit(solution)/shard_map/ppermute | solution.py:115
  109.7 0.4 fusion.50
  110.1 4.1 %collective-permute-done.6 = f32[3,4,64,64]{3,2,1,0:T(8,128)S(1)} collective-permute-done((f32[3,4,64,64]{3,2,1,0:T(8,128)S(1)}, f32[3,4,64,64]{3,2,1,0:T(8,128)S(1)}, u32[]{:S(2)}, u32[]{:S(2)}) %collective-permute-start.6) | collective-permute-done | bytes 196640 | tf_op jit(solution)/shard_map/ppermute | solution.py:115
  114.2 0.5 convolution_bitcast_fusion
  114.7 0.5 convolution_select_fusion
  115.5 0.3 fusion.19
  116.9 0.9 add_bitcast_fusion
  117.9 0.8 fusion.20
  118.7 1.0 fusion.1
  (59 shorter events, 4.5 us)
Async XLA Ops:
  7.2 67.1 %all-gather.3.cloned.1.call-start = ((), (), s32[]{:S(2)}) async-start(), calls=%async_computation | async-start | bytes 3538944 | tf_op jit(solution)/shard_map/all_gather | solution.py:12
  7.2 5.9 %copy-start.2 = (f32[1,4,64,128]{3,2,1,0:T(8,128)S(1)}, f32[1,4,64,128]{3,2,1,0:T(8,128)}, u32[]{:S(2)}) copy-start(f32[1,4,64,128]{3,2,1,0:T(8,128)} %param.14) | copy-start | bytes 393220
  8.6 9.9 %copy-start.8 = (s32[4,2]{0,1:T(2,128)S(1)}, s32[4,2]{0,1:T(2,128)}, u32[]{:S(2)}) copy-start(s32[4,2]{0,1:T(2,128)} %param.17) | copy-start | bytes 100
  12.1 64.4 %copy-start.1 = (f32[3,4,64,64]{3,2,1,0:T(8,128)S(1)}, f32[3,4,64,64]{3,2,1,0:T(8,128)}, u32[]{:S(2)}) copy-start(f32[3,4,64,64]{3,2,1,0:T(8,128)} %param.15) | copy-start | bytes 589828
  12.2 64.4 %copy-start.7 = (f32[1,4]{1,0:T(1,128)S(1)}, f32[1,4]{1,0:T(1,128)}, u32[]{:S(2)}) copy-start(f32[1,4]{1,0:T(1,128)} %param.16) | copy-start | bytes 52
  12.2 64.4 %copy-start = (f32[64,64,1]{1,0,2:T(8,128)S(1)}, f32[64,64,1]{1,0,2:T(8,128)}, u32[]{:S(2)}) copy-start(f32[64,64,1]{1,0,2:T(8,128)} %constant.92) | copy-start | bytes 49156
  13.3 7.4 %collective-permute-start = (f32[4,64,3]{2,1,0:T(8,128)S(1)}, f32[4,64,3]{2,1,0:T(8,128)S(1)}, u32[]{:S(2)}, u32[]{:S(2)}) collective-permute-start(f32[4,64,3]{2,1,0:T(8,128)S(1)} %get-tuple-element.23), channel_id=1, source_target_pairs={{0,4},{1,5},{2,6},{3,7},{8,12},{9,13},{10,14},{11,15},{16,20},{17,... | collective-permute-start | bytes 9224 | tf_op jit(solution)/shard_map/ppermute | solution.py:49
  17.2 5.7 %collective-permute-start.1 = (f32[4,64,3]{2,1,0:T(8,128)S(1)}, f32[4,64,3]{2,1,0:T(8,128)S(1)}, u32[]{:S(2)}, u32[]{:S(2)}) collective-permute-start(f32[4,64,3]{2,1,0:T(8,128)S(1)} %get-tuple-element.24), channel_id=1, source_target_pairs={{4,0},{5,1},{6,2},{7,3},{12,8},{13,9},{14,10},{15,11},{20,16},{21,... | collective-permute-start | bytes 9224 | tf_op jit(solution)/shard_map/ppermute | solution.py:50
  23.0 61.7 %collective-permute-start.2 = (f32[4,3,134]{2,1,0:T(4,128)S(1)}, f32[4,3,134]{2,1,0:T(4,128)S(1)}, u32[]{:S(2)}, u32[]{:S(2)}) collective-permute-start(f32[4,3,134]{2,1,0:T(4,128)S(1)} %get-tuple-element.10), channel_id=1, source_target_pairs={{0,1},{1,2},{2,3},{4,5},{5,6},{6,7},{8,9},{9,10},{10,11},{12,13},{... | collective-permute-start | bytes 19304 | tf_op jit(solution)/shard_map/ppermute | solution.py:49
  26.2 58.5 %collective-permute-start.3 = (f32[4,3,134]{2,1,0:T(4,128)S(1)}, f32[4,3,134]{2,1,0:T(4,128)S(1)}, u32[]{:S(2)}, u32[]{:S(2)}) collective-permute-start(f32[4,3,134]{2,1,0:T(4,128)S(1)} %get-tuple-element.11), channel_id=1, source_target_pairs={{1,0},{2,1},{3,2},{5,4},{6,5},{7,6},{9,8},{10,9},{11,10},{13,12},{... | collective-permute-start | bytes 19304 | tf_op jit(solution)/shard_map/ppermute | solution.py:50
  74.2 4.1 %copy-start.3 = (f32[64,64,1]{1,0,2:T(8,128)S(1)}, f32[64,64,1]{1,0,2:T(8,128)}, u32[]{:S(2)}) copy-start(f32[64,64,1]{1,0,2:T(8,128)} %constant.93) | copy-start | bytes 49156
  76.5 12.5 %copy-start.4 = (f32[64,64]{1,0:T(8,128)S(1)}, f32[64,64]{1,0:T(8,128)}, u32[]{:S(2)}) copy-start(f32[64,64]{1,0:T(8,128)} %constant.86.clone) | copy-start | bytes 49156
  76.5 12.5 %copy-start.5 = (f32[64,64]{1,0:T(8,128)S(1)}, f32[64,64]{1,0:T(8,128)}, u32[]{:S(2)}) copy-start(f32[64,64]{1,0:T(8,128)} %constant.87.clone) | copy-start | bytes 49156
  78.9 10.1 %collective-permute-start.4 = (f32[3,4,64,64]{3,2,1,0:T(8,128)S(1)}, f32[3,4,64,64]{3,2,1,0:T(8,128)S(1)}, u32[]{:S(2)}, u32[]{:S(2)}) collective-permute-start(f32[3,4,64,64]{3,2,1,0:T(8,128)S(1)} %pad_maximum_fusion.1), channel_id=1, source_target_pairs={{0,8},{8,16},{16,24},{1,9},{9,17},{17,25},{2,10},{10,18},{18,26},{... | collective-permute-start | bytes 589832 | tf_op jit(solution)/shard_map/ppermute | solution.py:115
  92.5 9.1 %collective-permute-start.5 = (f32[3,4,64,64]{3,2,1,0:T(8,128)S(1)}, f32[3,4,64,64]{3,2,1,0:T(8,128)S(1)}, u32[]{:S(2)}, u32[]{:S(2)}) collective-permute-start(f32[3,4,64,64]{3,2,1,0:T(8,128)S(1)} %pad_maximum_fusion.2), channel_id=1, source_target_pairs={{0,8},{8,16},{16,24},{1,9},{9,17},{17,25},{2,10},{10,18},{18,26},{... | collective-permute-start | bytes 589832 | tf_op jit(solution)/shard_map/ppermute | solution.py:115
  105.1 9.1 %collective-permute-start.6 = (f32[3,4,64,64]{3,2,1,0:T(8,128)S(1)}, f32[3,4,64,64]{3,2,1,0:T(8,128)S(1)}, u32[]{:S(2)}, u32[]{:S(2)}) collective-permute-start(f32[3,4,64,64]{3,2,1,0:T(8,128)S(1)} %pad_maximum_fusion.3), channel_id=1, source_target_pairs={{0,8},{8,16},{16,24},{1,9},{9,17},{17,25},{2,10},{10,18},{18,26},{... | collective-permute-start | bytes 589832 | tf_op jit(solution)/shard_map/ppermute | solution.py:115
  110.1 7.8 %copy-start.6 = (f32[256,256]{1,0:T(8,128)S(1)}, f32[256,256]{1,0:T(8,128)}, u32[]{:S(2)}) copy-start(f32[256,256]{1,0:T(8,128)} %constant.85.clone) | copy-start | bytes 786436
Sparse Core Ops, SparseCore 0:
  13.3 60.9 all-gather.2
